TPU v7x, 32 devices: a whole 2x2x4 slice. The times are simulated.
32 devices in a mesh: blk: 8 (over y, x, core), line: 4 (over z).
Axes of the slice: x: 2, y: 2, z: 4, core: 2. Of those that a mesh axis runs over, the one named last changes fastest.
Arguments:
- state: bfloat16 [32, 88, 256, 128], P('blk', None, 'line'), may hold values from -6 to 6
- speed_in: float32 [32, 256, 128], P('blk', 'line'), may hold values from -1 to 1
- speed_wall: float32 [32, 256, 128], P('blk', 'line'), may hold values from -1 to 1
- density: float32 [32, 256, 128], P('blk', 'line'), may hold values from 0.3 to 3
- rates: bfloat16 [88, 88], replicated, may hold values from -0.625 to 0.625
- wall_op: bfloat16 [256, 256], replicated, may hold values from -0.375 to 0.375
- block_perm: int32 [32], replicated, may hold values from 0 to 31, each once
- patch_src: int32 [32, 2, 16], P('blk', None, 'line'), may hold values from 0 to 63
- patch_flip: int32 [32, 2, 16], P('blk', None, 'line'), may hold values 0 or 1
- patch_wall: int32 [32, 2, 16], P('blk', None, 'line'), may hold values 0 or 1
Outputs:
- next_state: bfloat16 [32, 88, 256, 128], P('blk', None, 'line')
Inputs may be any that keep to these rules, and one draw needn't show every extreme that they name: `block_perm`: each block id 0 to 31 stands in exactly one slot. patch_src // 2 is a block id (not a slot) and patch_src % 2 its face; a patch's rows are the same rows of the source face. `patch_flip`: 1 reverses the order of a patch's rows. `patch_wall`: 1 mirrors the face's own cells in place of a neighbour's.
All inputs are finite; a program needn't handle non-finite values. No bound on the sum of `patch_flip` or of `patch_wall` on one device may be relied on, other than what follows from the above.
Results may differ from a plain program's by a relative error of at most 0.0014.
Values may be sent and summed in bfloat16 or wider, within the bound.
No kernel may reach another device: no remote copies, remote signals or barrier semaphores. Data moves between devices by JAX's collectives and lax.ppermute only.
A program may use at most 192 MiB of HBM per device.

v0:
```python
import math
import jax
import jax.numpy as jnp
from jax import lax
from jax.sharding import PartitionSpec as P

filter_sigma = 0.5
section_step = 0.25
deriv_coef = [5.0 / 6.0, -5.0 / 21.0, 5.0 / 84.0, -5.0 / 504.0, 1.0 / 1260.0]
high_pass = [(-1) ** offset * math.comb(10, 5 + offset) / 1024.0 for offset in range(-5, 6)]


def edge_cells(field):
    columns = field.shape[-1]
    return jnp.stack([field[..., :5], jnp.flip(field[..., columns - 5 :], -1)], 1)


def source_faces(block_perm, patch_src, patch_wall, first_slot):
    nblocks = block_perm.shape[0]
    block_ids = jnp.arange(nblocks, dtype=jnp.int32)
    matches = block_perm[None, :] == block_ids[:, None]
    slot_of = jnp.sum(jnp.where(matches, block_ids[None, :], 0), axis=1)
    owned = patch_src.shape[0]
    own_face = (first_slot + jnp.arange(owned, dtype=jnp.int32))[:, None, None] * 2 + jnp.arange(
        2, dtype=jnp.int32
    )[None, :, None]
    remote = jnp.take(slot_of, patch_src // 2) * 2 + patch_src % 2
    return jnp.where(patch_wall == 1, own_face, remote)


def select_ghosts(gathered, source, flips, patch_count):
    total = gathered.shape[0]
    chans = gathered.shape[2]
    rows = gathered.shape[3]
    flat = gathered.reshape(total * 2, chans, patch_count, rows // patch_count, 5)
    patch_index = jnp.arange(patch_count, dtype=jnp.int32)[None, None, :]
    picked = flat[source, :, patch_index]
    picked = jnp.where(flips[..., None, None, None] == 1, jnp.flip(picked, -2), picked)
    picked = jnp.transpose(picked, (0, 1, 3, 2, 4, 5))
    return picked.reshape(source.shape[0], 2, chans, rows, 5)


def section_update(state, ghosts, normal, speed_in, speed_wall, density, rates):
    values = state.astype(jnp.float32)
    columns = values.shape[-1]
    extended = jnp.concatenate(
        [jnp.flip(ghosts[:, 0].astype(jnp.float32), -1), values, ghosts[:, 1].astype(jnp.float32)],
        -1,
    )
    smooth = values
    for offset in range(11):
        smooth = (
            smooth - filter_sigma * high_pass[offset] * extended[..., offset : offset + columns]
        )
    slope = jnp.zeros_like(values)
    for offset in range(1, 6):
        slope = slope + deriv_coef[offset - 1] * (
            extended[..., 5 + offset : 5 + offset + columns]
            - extended[..., 5 - offset : 5 - offset + columns]
        )
    mixed = jnp.einsum("ce,belp->bclp", rates, state, preferred_element_type=jnp.float32)
    residual = -speed_in[:, None] * slope - speed_wall[:, None] * normal + density[:, None] * mixed
    return (smooth + section_step * residual).astype(jnp.bfloat16)


def body(
    state,
    speed_in,
    speed_wall,
    density,
    rates,
    wall_op,
    block_perm,
    patch_src,
    patch_flip,
    patch_wall,
):
    owned = state.shape[0]
    rows = state.shape[2]
    gathered = lax.all_gather(edge_cells(state), "blk", axis=0, tiled=True)
    source = source_faces(block_perm, patch_src, patch_wall, lax.axis_index("blk") * owned)
    ghosts = select_ghosts(gathered, source, patch_flip, patch_src.shape[2])
    first_row = lax.axis_index("line") * rows
    my_rows = lax.dynamic_slice_in_dim(wall_op, first_row, rows, 0)
    summed = jnp.einsum(
        "lm,bcmp->bclp",
        my_rows,
        lax.all_gather(state, "line", axis=2, tiled=True),
        preferred_element_type=jnp.float32,
    )
    normal = lax.optimization_barrier(summed.astype(jnp.bfloat16))
    return section_update(
        state, ghosts, normal.astype(jnp.float32), speed_in, speed_wall, density, rates
    )


def solution(mesh):
    return jax.shard_map(
        body,
        mesh=mesh,
        in_specs=(
            P("blk", None, "line", None),
            P("blk", "line", None),
            P("blk", "line", None),
            P("blk", "line", None),
            P(),
            P(),
            P(),
            P("blk", None, "line"),
            P("blk", None, "line"),
            P("blk", None, "line"),
        ),
        out_specs=P("blk", None, "line", None),
        check_vma=False,
    )
```

profile of v0, /device:TPU:0, one launch (start us, length us, event | category | flops | bytes accessed | tf_op | source)
XLA Modules:
  0.0 582.6 jit_solution(9919181915388642683)
XLA Ops:
  6.5 10.9 %fusion.21 = (bf16[4,88,64,5]{3,2,1,0:T(8,128)(2,1)}, bf16[4,88,64,5]{3,2,1,0:T(8,128)(2,1)}) fusion(bf16[4,88,64,128]{3,2,1,0:T(8,128)(2,1)} %param.10), kind=kLoop, calls=%fused_computation.67 | loop fusion | bytes 901120 | tf_op jit(solution)/shard_map/slice | solution.py:15
  17.5 8.2 %copy.32 = bf16[4,88,64,5]{1,2,3,0:T(8,128)(2,1)S(1)} copy(bf16[4,88,64,5]{3,2,1,0:T(8,128)(2,1)} %get-tuple-element.8) | data formatting | bytes 450560
  25.7 8.2 %copy.31 = bf16[4,88,64,5]{1,2,3,0:T(8,128)(2,1)S(1)} copy(bf16[4,88,64,5]{3,2,1,0:T(8,128)(2,1)} %get-tuple-element.7) | data formatting | bytes 450560
  33.9 1.0 pad_maximum_fusion.2
  34.8 0.0 all-gather.3.cloned.1.call-update
  34.9 0.0 copy-start.5
  34.9 0.0 copy-start.8
  34.9 0.2 all-gather.5.cloned.1.call-start
  35.1 0.5 all-gather.5.cloned.1.call-update
  35.6 0.0 copy-start.7
  35.7 0.0 copy-start.3
  35.7 0.0 copy-start.6
  35.7 0.0 copy-start.4
  35.7 8.2 %convert_element_type.27 = f32[4,88,64,128]{3,2,1,0:T(8,128)} convert(bf16[4,88,64,128]{3,2,1,0:T(8,128)(2,1)} %param.10) | non-fusion elementwise | flops 2883584 | bytes 17301504 | tf_op jit(solution)/shard_map/convert_element_type | solution.py:44
  44.0 0.1 reshape.61
  44.1 0.1 select_reduce_fusion
  44.2 0.7 gather_fusion
  44.9 0.1 reshape.60
  45.0 0.1 iota_add_fusion
  45.0 0.1 bitcast_or_fusion
  45.1 0.1 reshape.67
  45.3 11.3 %fusion.13 = f32[4,64,128,88]{2,3,1,0:T(8,128)} fusion(bf16[4,88,64,128]{3,2,1,0:T(8,128)(2,1)} %param.10, bf16[88,88]{1,0:T(8,128)(2,1)S(1)} %copy-done.4), kind=kOutput, calls=%fused_computation.37 | convolution fusion | flops 507510784 | bytes 17316992 | tf_op jit(solution)/shard_map/ce,belp->bclp/dot_general | solution.py:61
  56.6 22.2 %all-gather.3.cloned.1.call-done = bf16[32,2,88,64,5]{2,3,4,1,0:T(8,128)(2,1)} async-done(((bf16[4,2,88,64,5]{2,3,4,1,0:T(8,128)(2,1)}), bf16[32,2,88,64,5]{2,3,4,1,0:T(8,128)(2,1)}) %all-gather.3.cloned.1.call-update) | async-done | bytes 3604496 | tf_op jit(solution)/shard_map/all_gather | solution.py:80
  78.7 3.2 gather_fusion.1
  82.0 0.8 rev.13
  82.8 0.1 select_bitcast_fusion
  82.9 19.2 %copy.26 = bf16[4,2,88,4,16,5]{5,4,3,2,0,1:T(8,128)(2,1)} copy(bf16[4,2,88,4,16,5]{2,4,5,3,1,0:T(8,128)(2,1)S(1)} %select_bitcast_fusion) | data formatting | bytes 901120 | tf_op jit(solution)/shard_map/transpose | solution.py:39
  102.1 12.3 %fusion.12 = (f32[4,88,64,5]{3,2,1,0:T(8,128)}, f32[4,88,64,5]{3,2,1,0:T(8,128)}) fusion(bf16[4,2,88,64,5]{4,3,2,0,1:T(8,128)(2,1)} %bitcast.45), kind=kLoop, calls=%fused_computation.36 | loop fusion | flops 225280 | bytes 1351680 | tf_op jit(solution)/shard_map/convert_element_type | solution.py:47
  114.4 17.6 %rev.14 = f32[4,88,64,5]{3,2,1,0:T(8,128)} reverse(f32[4,88,64,5]{3,2,1,0:T(8,128)} %get-tuple-element.5), dimensions={3} | reverse | bytes 901120 | tf_op jit(solution)/shard_map/jit(_flip)/rev | solution.py:47
  132.1 339.3 %all-gather.5.cloned.1.call-done = bf16[4,88,256,128]{3,2,1,0:T(8,128)(2,1)} async-done(((bf16[4,88,64,128]{3,2,1,0:T(8,128)(2,1)}), bf16[4,88,256,128]{3,2,1,0:T(8,128)(2,1)}) %all-gather.5.cloned.1.call-update) | async-done | bytes 23068688 | tf_op jit(solution)/shard_map/all_gather | solution.py:88
  471.4 11.7 %convert_bitcast_fusion = bf16[4,88,64,128]{3,2,1,0:T(8,128)(2,1)S(1)} fusion(bf16[4,88,256,128]{3,2,1,0:T(8,128)(2,1)} %all-gather.5.cloned.1.call-done, bf16[256,256]{1,0:T(8,128)(2,1)S(1)} %copy-done, s32[]{:T(128)S(6)} %select_n.47), kind=kOutput, calls=%fused_computation.39 | convolution fusion | flops 1479278592 | bytes 28868612 | tf_op jit(solution)/shard_map/lm,bcmp->bclp/dot_general | solution.py:85
  483.1 92.7 %fusion.10 = bf16[4,88,64,128]{3,2,1,0:T(8,128)(2,1)} fusion(f32[4,64,128,88]{2,3,1,0:T(8,128)} %fusion.13, bf16[4,88,64,128]{3,2,1,0:T(8,128)(2,1)S(1)} %convert_bitcast_fusion, f32[4,88,64,5]{3,2,1,0:T(8,128)} %get-tuple-element.6, f32[4,88,64,128]{3,2,1,0:T(8,128)} %convert_element_type.27, f32[4,88,64,5]{3,2,1,0:T(8,128)} %rev.14, ...), kind=kLoop, calls=%fused_computation.31 | loop fusion | flops 158597120 | bytes 35897344 | tf_op jit(solution)/shard_map/convert_element_type | solution.py:63
  (19 shorter events, 0.1 us)
Async XLA Ops:
  6.5 464.9 %copy-start = (bf16[256,256]{1,0:T(8,128)(2,1)S(1)}, bf16[256,256]{1,0:T(8,128)(2,1)}, u32[]{:S(2)}) copy-start(bf16[256,256]{1,0:T(8,128)(2,1)} %param.15) | copy-start | bytes 393220
  6.5 72.2 %all-gather.3.cloned.1.call-start = ((), (), s32[]{:S(2)}) async-start(), calls=%async_computation | async-start | bytes 5898240 | tf_op jit(solution)/shard_map/all_gather | solution.py:80
  34.9 9.1 %copy-start.5 = (s32[4,2,4]{2,1,0:T(2,128)S(1)}, s32[4,2,4]{2,1,0:T(2,128)}, u32[]{:S(2)}) copy-start(s32[4,2,4]{2,1,0:T(2,128)} %param.17) | copy-start | bytes 388
  34.9 9.2 %copy-start.8 = (s32[32]{0:T(128)S(1)}, s32[32]{0:T(128)}, u32[]{:S(2)}) copy-start(s32[32]{0:T(128)} %param.16) | copy-start | bytes 388
  34.9 436.5 %all-gather.5.cloned.1.call-start = ((), (), s32[]{:S(2)}) async-start(), calls=%async_computation.1 | async-start | bytes 28835840 | tf_op jit(solution)/shard_map/all_gather | solution.py:88
  35.6 9.4 %copy-start.7 = (s32[4,2,4]{2,1,0:T(2,128)S(1)}, s32[4,2,4]{2,1,0:T(2,128)}, u32[]{:S(2)}) copy-start(s32[4,2,4]{2,1,0:T(2,128)} %param.19) | copy-start | bytes 388
  35.7 9.6 %copy-start.3 = (f32[4,64,128]{2,1,0:T(8,128)S(1)}, f32[4,64,128]{2,1,0:T(8,128)}, u32[]{:S(2)}) copy-start(f32[4,64,128]{2,1,0:T(8,128)} %param.11) | copy-start | bytes 393220
  35.7 9.6 %copy-start.6 = (s32[4,2,4]{2,1,0:T(2,128)S(1)}, s32[4,2,4]{2,1,0:T(2,128)}, u32[]{:S(2)}) copy-start(s32[4,2,4]{2,1,0:T(2,128)} %param.18) | copy-start | bytes 388
  35.7 9.6 %copy-start.4 = (bf16[88,88]{1,0:T(8,128)(2,1)S(1)}, bf16[88,88]{1,0:T(8,128)(2,1)}, u32[]{:S(2)}) copy-start(bf16[88,88]{1,0:T(8,128)(2,1)} %param.14) | copy-start | bytes 46468
  132.1 351.0 %copy-start.1 = (f32[4,64,128]{2,1,0:T(8,128)S(1)}, f32[4,64,128]{2,1,0:T(8,128)}, u32[]{:S(2)}) copy-start(f32[4,64,128]{2,1,0:T(8,128)} %param.13) | copy-start | bytes 393220
  132.1 351.0 %copy-start.2 = (f32[4,64,128]{2,1,0:T(8,128)S(1)}, f32[4,64,128]{2,1,0:T(8,128)}, u32[]{:S(2)}) copy-start(f32[4,64,128]{2,1,0:T(8,128)} %param.12) | copy-start | bytes 393220
Sparse Core Ops, SparseCore 0:
  35.0 43.6 all-gather.2
  80.3 391.0 all-gather.4
where the time goes:
time: 583 us
  waiting for transfers between devices  362 us (62%)
  other arithmetic  115 us (20%)
  local copies, waits for them, and re-layouts  69.1 us (12%)
  matrix products  23 us (4%)
  between operations  13.6 us (2%)
    all_gather x1, waiting for transfers between devices, body(): lax.all_gather(state, 'line', axis=2, tiled=True)  339 us
    convert_element_type x1, other arithmetic, section_update(): return (smooth + section_step * residual).astype(jnp.bfloat16)  92.7 us
    all_gather x1, waiting for transfers between devices, body(): gathered = lax.all_gather(edge_cells(state), 'blk', axis=0, tiled=True)  22.2 us
    transpose x1, local copies, waits for them, and re-layouts, select_ghosts(): picked = jnp.transpose(picked, (0, 1, 3, 2, 4, 5))  19.2 us
    rev x1, local copies, waits for them, and re-layouts, section_update(): jnp.flip(ghosts[:, 0].astype(jnp.float32), -1)  17.6 us
    unnamed x20, local copies, waits for them, and re-layouts  16.4 us
    convert_element_type x1, other arithmetic, section_update(): ghosts[:, 0].astype(jnp.float32)  12.3 us
    dot_general x1, matrix products, body(): jnp.einsum('lm,bcmp->bclp', my_rows, lax.all_gather(state, 'line', axis=2...  11.7 us
  transfers between devices with their start and end apart: 2, of which 2 were waited for; matrix products, arithmetic and copies ran while one was open for 13% of the time, Pallas kernels for 0%

commit v1 on v0

--- a/solution.py
+++ b/solution.py
@@ -8,6 +8,22 @@
 section_step = 0.25
 deriv_coef = [5.0 / 6.0, -5.0 / 21.0, 5.0 / 84.0, -5.0 / 504.0, 1.0 / 1260.0]
 high_pass = [(-1) ** offset * math.comb(10, 5 + offset) / 1024.0 for offset in range(-5, 6)]
+
+
+def ring_product(value, axis, dim, contribution):
+    size, index, rows = (lax.axis_size(axis), lax.axis_index(axis), value.shape[dim])
+    upward = [(i, (i + 1) % size) for i in range(size)]
+    behind = [(i, (i - 1) % size) for i in range(size)]
+    half = size // 2
+    from_left = from_right = value
+    total = contribution(value, index * rows)
+    for lap in range(1, half + 1):
+        from_left = lax.ppermute(from_left, axis, upward)
+        if lap < size - half:
+            from_right = lax.ppermute(from_right, axis, behind)
+            total = total + contribution(from_right, (index + lap) % size * rows)
+        total = total + contribution(from_left, (index - lap) % size * rows)
+    return total
 
 
 def edge_cells(field):
@@ -82,11 +98,16 @@
     ghosts = select_ghosts(gathered, source, patch_flip, patch_src.shape[2])
     first_row = lax.axis_index("line") * rows
     my_rows = lax.dynamic_slice_in_dim(wall_op, first_row, rows, 0)
-    summed = jnp.einsum(
-        "lm,bcmp->bclp",
-        my_rows,
-        lax.all_gather(state, "line", axis=2, tiled=True),
-        preferred_element_type=jnp.float32,
+    summed = ring_product(
+        state,
+        "line",
+        2,
+        lambda own_block, at: jnp.einsum(
+            "lm,bcmp->bclp",
+            lax.dynamic_slice_in_dim(my_rows, at, own_block.shape[2], axis=1),
+            own_block,
+            preferred_element_type=jnp.float32,
+        ),
     )
     normal = lax.optimization_barrier(summed.astype(jnp.bfloat16))
     return section_update(

time: 583 us -> 505 us (0.87)
  waiting for transfers between devices: 362 us -> 246 us
  matrix products: 23 us -> 51.2 us
    all_gather x1 -> x0, waiting for transfers between devices: 339 us -> none  [body(): lax.all_gather(state, 'line', axis=2, tiled=True)]
    ppermute x0 -> x3, waiting for transfers between devices: none -> 246 us  [the longest x2 160 us: ring_product(): from_left = lax.ppermute(from_left, axis, upward)]
    dot_general x1 -> x4, matrix products: 11.7 us -> 42.7 us  [body(): jnp.einsum('lm,bcmp->bclp', lax.dynamic_slice_in_dim(my_rows, at, own_blo...]
    all_gather x1, waiting for transfers between devices: 22.2 us -> 0.01 us  [body(): gathered = lax.all_gather(edge_cells(state), 'blk', axis=0, tiled=True)]
    unnamed x20 -> x24, local copies, waits for them, and re-layouts: 16.4 us -> 16.4 us
  transfers between devices with their start and end apart: 2 -> 4, of which waited for: 2 -> 3; matrix products, arithmetic and copies ran while one was open for 13% -> 25% of each run, Pallas kernels for 0% -> 0%
where the time goes in v1:
time: 505 us; the launch traced here: 504 us
  waiting for transfers between devices  246 us (49%)
  other arithmetic  119 us (24%)
  local copies, waits for them, and re-layouts  69.1 us (14%)
  matrix products  51.2 us (10%)
  between operations  13.6 us (3%)
  starting transfers between devices  5.09 us (1%)
    ppermute x2, waiting for transfers between devices, ring_product(): from_left = lax.ppermute(from_left, axis, upward)  160 us
    convert_element_type x1, other arithmetic, section_update(): return (smooth + section_step * residual).astype(jnp.bfloat16)  97.2 us
    ppermute x1, waiting for transfers between devices, ring_product(): from_right = lax.ppermute(from_right, axis, behind)  86.9 us
    dot_general x4, matrix products, body(): jnp.einsum('lm,bcmp->bclp', lax.dynamic_slice_in_dim(my_rows, at, own_blo...  42.7 us
    transpose x1, local copies, waits for them, and re-layouts, select_ghosts(): picked = jnp.transpose(picked, (0, 1, 3, 2, 4, 5))  19.2 us
    rev x1, local copies, waits for them, and re-layouts, section_update(): jnp.flip(ghosts[:, 0].astype(jnp.float32), -1)  17.6 us
    unnamed x24, local copies, waits for them, and re-layouts  16.4 us
    convert_element_type x1, other arithmetic, section_update(): ghosts[:, 0].astype(jnp.float32)  12 us
  transfers between devices with their start and end apart: 4, of which 3 were waited for; matrix products, arithmetic and copies ran while one was open for 25% of the time, Pallas kernels for 0%

profile of v1, /device:TPU:0, one launch (start us, length us, event | category | flops | bytes accessed | tf_op | source)
XLA Modules:
  0.0 504.4 jit_solution(12324888717607153495)
XLA Ops:
  6.5 3.1 collective-permute-start.1
  9.6 2.0 collective-permute-start
  11.6 10.9 %fusion.30 = (bf16[4,88,64,5]{3,2,1,0:T(8,128)(2,1)}, bf16[4,88,64,5]{3,2,1,0:T(8,128)(2,1)}) fusion(bf16[4,88,64,128]{3,2,1,0:T(8,128)(2,1)} %param.10), kind=kLoop, calls=%fused_computation.76 | loop fusion | bytes 901120 | tf_op jit(solution)/shard_map/slice | solution.py:31
  22.6 8.2 %copy.35 = bf16[4,88,64,5]{1,2,3,0:T(8,128)(2,1)S(1)} copy(bf16[4,88,64,5]{3,2,1,0:T(8,128)(2,1)} %get-tuple-element.8) | data formatting | bytes 450560
  30.7 8.2 %copy.34 = bf16[4,88,64,5]{1,2,3,0:T(8,128)(2,1)S(1)} copy(bf16[4,88,64,5]{3,2,1,0:T(8,128)(2,1)} %get-tuple-element.7) | data formatting | bytes 450560
  38.9 0.0 copy-start.5
  39.0 1.0 pad_maximum_fusion.2
  40.0 0.0 all-gather.2.cloned.1.call-update
  40.0 97.1 %collective-permute-done.1 = bf16[4,88,64,128]{3,2,1,0:T(8,128)(2,1)} collective-permute-done((bf16[4,88,64,128]{3,2,1,0:T(8,128)(2,1)}, bf16[4,88,64,128]{3,2,1,0:T(8,128)(2,1)}, u32[]{:S(2)}, u32[]{:S(2)}) %collective-permute-start.1) | collective-permute-done | bytes 5767200 | tf_op jit(solution)/shard_map/ppermute | solution.py:21
  137.1 8.4 %convert_element_type.27 = f32[4,88,64,128]{3,2,1,0:T(8,128)} convert(bf16[4,88,64,128]{3,2,1,0:T(8,128)(2,1)} %param.10) | non-fusion elementwise | flops 2883584 | bytes 17301504 | tf_op jit(solution)/shard_map/convert_element_type | solution.py:60
  145.5 0.1 reshape.61
  145.6 0.1 select_reduce_fusion
  145.7 0.7 gather_fusion
  146.4 0.1 reshape.60
  146.5 0.1 iota_add_fusion
  146.6 0.1 bitcast_or_fusion
  146.7 0.1 reshape.67
  146.8 0.0 slice-start.1
  146.8 8.7 %fusion.22 = f32[64,4,88,128]{3,0,2,1:T(8,128)} fusion(bf16[4,88,64,128]{3,2,1,0:T(8,128)(2,1)} %param.10, bf16[256,256]{1,0:T(8,128)(2,1)S(1)} %copy-done, s32[]{:T(128)S(6)} %select_n.80), kind=kOutput, calls=%fused_computation.50 | convolution fusion | flops 369098752 | bytes 17317892 | tf_op jit(solution)/shard_map/lm,bcmp->bclp/dot_general | solution.py:105
  155.6 8.5 %fusion.14 = f32[4,64,128,88]{2,3,1,0:T(8,128)} fusion(bf16[4,88,64,128]{3,2,1,0:T(8,128)(2,1)S(1)} %bitcast.64, bf16[88,88]{1,0:T(8,128)(2,1)S(1)} %copy-done.4), kind=kOutput, calls=%fused_computation.39 | convolution fusion | flops 507510784 | bytes 17316992 | tf_op jit(solution)/shard_map/ce,belp->bclp/dot_general | solution.py:77
  164.1 8.5 %fusion.18 = f32[64,4,88,128]{3,0,2,1:T(8,128)} fusion(bf16[4,88,64,128]{3,2,1,0:T(8,128)(2,1)} %collective-permute-done.1, bf16[256,256]{1,0:T(8,128)(2,1)S(1)} %copy-done, s32[]{:T(128)S(6)} %select_n.80, s32[]{:T(128)S(6)} %select_n.86), kind=kOutput, calls=%fused_computation.46 | convolution fusion | flops 369098752 | bytes 17317896 | tf_op jit(solution)/shard_map/lm,bcmp->bclp/dot_general | solution.py:105
  172.6 86.9 %collective-permute-done = bf16[4,88,64,128]{3,2,1,0:T(8,128)(2,1)} collective-permute-done((bf16[4,88,64,128]{3,2,1,0:T(8,128)(2,1)}, bf16[4,88,64,128]{3,2,1,0:T(8,128)(2,1)}, u32[]{:S(2)}, u32[]{:S(2)}) %collective-permute-start) | collective-permute-done | bytes 5767200 | tf_op jit(solution)/shard_map/ppermute | solution.py:23
  259.5 8.5 %fusion.20 = f32[64,4,88,128]{3,0,2,1:T(8,128)} fusion(bf16[4,88,64,128]{3,2,1,0:T(8,128)(2,1)} %collective-permute-done, bf16[256,256]{1,0:T(8,128)(2,1)S(1)} %copy-done, s32[]{:T(128)S(6)} %select_n.80, s32[]{:T(128)S(6)} %select_n.83), kind=kOutput, calls=%fused_computation.48 | convolution fusion | flops 369098752 | bytes 17317896 | tf_op jit(solution)/shard_map/lm,bcmp->bclp/dot_general | solution.py:105
  268.0 3.2 gather_fusion.1
  271.2 0.8 rev.13
  272.0 0.1 select_bitcast_fusion
  272.2 19.2 %copy.26 = bf16[4,2,88,4,16,5]{5,4,3,2,0,1:T(8,128)(2,1)} copy(bf16[4,2,88,4,16,5]{2,4,5,3,1,0:T(8,128)(2,1)S(1)} %select_bitcast_fusion) | data formatting | bytes 901120 | tf_op jit(solution)/shard_map/transpose | solution.py:55
  291.4 12.0 %fusion.13 = (f32[4,88,64,5]{3,2,1,0:T(8,128)}, f32[4,88,64,5]{3,2,1,0:T(8,128)}) fusion(bf16[4,2,88,64,5]{4,3,2,0,1:T(8,128)(2,1)} %bitcast.65), kind=kLoop, calls=%fused_computation.38 | loop fusion | flops 225280 | bytes 1351680 | tf_op jit(solution)/shard_map/convert_element_type | solution.py:63
  303.4 17.6 %rev.14 = f32[4,88,64,5]{3,2,1,0:T(8,128)} reverse(f32[4,88,64,5]{3,2,1,0:T(8,128)} %get-tuple-element.5), dimensions={3} | reverse | bytes 901120 | tf_op jit(solution)/shard_map/jit(_flip)/rev | solution.py:63
  321.0 62.5 %collective-permute-done.2 = bf16[4,88,64,128]{3,2,1,0:T(8,128)(2,1)} collective-permute-done((bf16[4,88,64,128]{3,2,1,0:T(8,128)(2,1)}, bf16[4,88,64,128]{3,2,1,0:T(8,128)(2,1)}, u32[]{:S(2)}, u32[]{:S(2)}) %collective-permute-start.2) | collective-permute-done | bytes 5767200 | tf_op jit(solution)/shard_map/ppermute | solution.py:21
  383.4 17.0 %fusion.11 = bf16[4,88,64,128]{3,2,1,0:T(8,128)(2,1)} fusion(f32[64,4,88,128]{3,0,2,1:T(8,128)} %fusion.18, f32[64,4,88,128]{3,0,2,1:T(8,128)} %fusion.22, f32[64,4,88,128]{3,0,2,1:T(8,128)} %fusion.20, bf16[4,88,64,128]{3,2,1,0:T(8,128)(2,1)} %collective-permute-done.2, bf16[256,256]{1,0:T(8,128)(2,1)S(1)} %copy-done, s32[]{:T(128)S(6)} %select_n.80, ...), kind=kOutput, calls=%fused_computation.34 | convolution fusion | flops 380633088 | bytes 46153736 | tf_op jit(solution)/shard_map/lm,bcmp->bclp/dot_general | solution.py:105
  400.4 97.2 %fusion.10 = bf16[4,88,64,128]{3,2,1,0:T(8,128)(2,1)} fusion(f32[4,64,128,88]{2,3,1,0:T(8,128)} %fusion.14, bf16[4,88,64,128]{3,2,1,0:T(8,128)(2,1)} %fusion.11, f32[4,88,64,5]{3,2,1,0:T(8,128)} %get-tuple-element.6, f32[4,88,64,128]{3,2,1,0:T(8,128)} %convert_element_type.27, f32[4,88,64,5]{3,2,1,0:T(8,128)} %rev.14, f32[4,64,128]{2,1,0:T(8,128)S(1)} %copy-done.1, ...), kind=kLoop, calls=%fused_computation.31 | loop fusion | flops 158597120 | bytes 35897344 | tf_op jit(solution)/shard_map/convert_element_type | solution.py:79
  (30 shorter events, 0.1 us)
Async XLA Ops:
  6.5 140.3 %copy-start = (bf16[256,256]{1,0:T(8,128)(2,1)S(1)}, bf16[256,256]{1,0:T(8,128)(2,1)}, u32[]{:S(2)}) copy-start(bf16[256,256]{1,0:T(8,128)(2,1)} %param.15) | copy-start | bytes 393220
  6.5 261.5 %all-gather.2.cloned.1.call-start = ((), (), s32[]{:S(2)}) async-start(), calls=%async_computation | async-start | bytes 5898240 | tf_op jit(solution)/shard_map/all_gather | solution.py:96
  6.5 130.6 %collective-permute-start.1 = (bf16[4,88,64,128]{3,2,1,0:T(8,128)(2,1)}, bf16[4,88,64,128]{3,2,1,0:T(8,128)(2,1)}, u32[]{:S(2)}, u32[]{:S(2)}) collective-permute-start(bf16[4,88,64,128]{3,2,1,0:T(8,128)(2,1)} %param.10), channel_id=1, source_target_pairs={{0,1},{1,2},{2,3},{3,0},{4,5},{5,6},{6,7},{7,4},{8,9},{9,10},{10,1... | collective-permute-start | bytes 17301512 | tf_op jit(solution)/shard_map/ppermute | solution.py:21
  9.6 249.9 %collective-permute-start = (bf16[4,88,64,128]{3,2,1,0:T(8,128)(2,1)}, bf16[4,88,64,128]{3,2,1,0:T(8,128)(2,1)}, u32[]{:S(2)}, u32[]{:S(2)}) collective-permute-start(bf16[4,88,64,128]{3,2,1,0:T(8,128)(2,1)} %param.10), channel_id=1, source_target_pairs={{0,3},{1,0},{2,1},{3,2},{4,7},{5,4},{6,5},{7,6},{8,11},{9,8},{10,9... | collective-permute-start | bytes 17301512 | tf_op jit(solution)/shard_map/ppermute | solution.py:23
  38.9 106.6 %copy-start.5 = (s32[4,2,4]{2,1,0:T(2,128)S(1)}, s32[4,2,4]{2,1,0:T(2,128)}, u32[]{:S(2)}) copy-start(s32[4,2,4]{2,1,0:T(2,128)} %param.17) | copy-start | bytes 388
  38.9 106.7 %copy-start.8 = (s32[32]{0:T(128)S(1)}, s32[32]{0:T(128)}, u32[]{:S(2)}) copy-start(s32[32]{0:T(128)} %param.16) | copy-start | bytes 388
  39.0 107.6 %copy-start.7 = (s32[4,2,4]{2,1,0:T(2,128)S(1)}, s32[4,2,4]{2,1,0:T(2,128)}, u32[]{:S(2)}) copy-start(s32[4,2,4]{2,1,0:T(2,128)} %param.19) | copy-start | bytes 388
  39.0 107.8 %copy-start.3 = (f32[4,64,128]{2,1,0:T(8,128)S(1)}, f32[4,64,128]{2,1,0:T(8,128)}, u32[]{:S(2)}) copy-start(f32[4,64,128]{2,1,0:T(8,128)} %param.11) | copy-start | bytes 393220
  40.0 106.8 %copy-start.6 = (s32[4,2,4]{2,1,0:T(2,128)S(1)}, s32[4,2,4]{2,1,0:T(2,128)}, u32[]{:S(2)}) copy-start(s32[4,2,4]{2,1,0:T(2,128)} %param.18) | copy-start | bytes 388
  137.1 246.3 %collective-permute-start.2 = (bf16[4,88,64,128]{3,2,1,0:T(8,128)(2,1)}, bf16[4,88,64,128]{3,2,1,0:T(8,128)(2,1)}, u32[]{:S(2)}, u32[]{:S(2)}) collective-permute-start(bf16[4,88,64,128]{3,2,1,0:T(8,128)(2,1)} %collective-permute-done.1), channel_id=1, source_target_pairs={{0,1},{1,2},{2,3},{3,0},{4,5},{5,6},{6,7},{7,4},{8,9},{9,10},{10,1... | collective-permute-start | bytes 17301512 | tf_op jit(solution)/shard_map/ppermute | solution.py:21
  145.5 10.1 %slice-start = ((s8[5767168]{0:T(1024)(128)(4,1)}), s8[1572864]{0:T(1024)(128)(4,1)S(1)}, s32[]{:S(2)}) async-start(s8[5767168]{0:T(1024)(128)(4,1)} %bitcast.63), calls=%async_computation.1 | async-start | bytes 3145728
  145.5 10.1 %copy-start.4 = (bf16[88,88]{1,0:T(8,128)(2,1)S(1)}, bf16[88,88]{1,0:T(8,128)(2,1)}, u32[]{:S(2)}) copy-start(bf16[88,88]{1,0:T(8,128)(2,1)} %param.14) | copy-start | bytes 46468
  146.8 8.7 %slice-start.1 = ((s8[5767168]{0:T(1024)(128)(4,1)}), s8[4194304]{0:T(1024)(128)(4,1)S(1)}, s32[]{:S(2)}) async-start(s8[5767168]{0:T(1024)(128)(4,1)} %bitcast.63), calls=%async_computation.2 | async-start | bytes 8388608
  321.0 79.4 %copy-start.1 = (f32[4,64,128]{2,1,0:T(8,128)S(1)}, f32[4,64,128]{2,1,0:T(8,128)}, u32[]{:S(2)}) copy-start(f32[4,64,128]{2,1,0:T(8,128)} %param.13) | copy-start | bytes 393220
  321.0 79.4 %copy-start.2 = (f32[4,64,128]{2,1,0:T(8,128)S(1)}, f32[4,64,128]{2,1,0:T(8,128)}, u32[]{:S(2)}) copy-start(f32[4,64,128]{2,1,0:T(8,128)} %param.12) | copy-start | bytes 393220
Sparse Core Ops, SparseCore 0:
  40.1 40.6 all-gather.1
